TPU v7x, 128 devices: a whole 4x4x4 slice. The times are simulated.
128 devices in a mesh: grp: 4 (over y), own: 32 (over x, z, core).
Axes of the slice: x: 4, y: 4, z: 4, core: 2. Of those that a mesh axis runs over, the one named last changes fastest.
Arguments:
- embeddings: float32 [98304, 768], P(('grp', 'own')), may hold values from -64 to 64
- cluster_ids: int32 [98304], P(('grp', 'own')), may hold values from 0 to 511, as said below
- owner_map: int32 [512], replicated, may hold values from 0 to 31, as said below
- source_order: int32 [98304], P(('grp', 'own')), may hold values from 0 to 767, as said below
Outputs:
- dup_score: float32 [98304], P(('grp', 'own'))
- centroids: float32 [512, 768], P('own')
Inputs may be any that keep to these rules, and one draw needn't show every extreme that they name: `owner_map`: every owner index is given to exactly 16 clusters. `cluster_ids`: within the 768 rows of one device, at most 48 rows have clusters of one owner index; in every draw some owner index receives exactly 48 rows from every device, and every device sends exactly 48 rows to some owner index. Cluster sizes are uneven and some clusters may be empty. `source_order`: each aligned block of 768 entries is a permutation of 0 to 767.
All inputs are finite; a program needn't handle non-finite values.
Results may differ from a plain program's by a relative error of at most 0.0003.
Values sent between devices are 32-bit elements; how exact they have to be, the bound alone decides.
A program may use at most 128 MiB of HBM per device.

v0:
```python
import jax
import jax.numpy as jnp
from jax import lax
from jax.sharding import PartitionSpec as P

CL_OWN = 16


sharpness = 6.0


def unit_rows(embeddings):
    squares = jnp.sum(embeddings * embeddings, axis=1, keepdims=True)
    return embeddings * lax.rsqrt(squares + 1e-06)


def owner_positions(owner_map):
    cluster_index = jnp.arange(owner_map.shape[0], dtype=jnp.int32)
    same_owner = owner_map[:, None] == owner_map[None, :]
    earlier = cluster_index[None, :] < cluster_index[:, None]
    before = jnp.sum((same_owner & earlier).astype(jnp.int32), axis=1)
    return owner_map * CL_OWN + before


def masked_weights(left_rows, left_ids, right_rows, right_ids):
    scores = jnp.einsum(
        "id,jd->ij",
        left_rows,
        right_rows,
        preferred_element_type=jnp.float32,
        precision=lax.Precision.HIGHEST,
    )
    linked = (left_ids[:, None] == right_ids[None, :]) & (left_ids[:, None] >= 0)
    return jnp.where(linked, jnp.exp(sharpness * (scores - 1.0)), 0.0)


def tile_sums(left_rows, left_ids, right_rows, right_ids):
    right_count = right_rows.shape[0]
    block_rows = 512
    block_count = right_count // block_rows
    right_blocks = right_rows.reshape(block_count, block_rows, right_rows.shape[1])
    id_blocks = right_ids.reshape(block_count, block_rows)

    def one_block(row_total, block_pair):
        weights = masked_weights(left_rows, left_ids, block_pair[0], block_pair[1])
        column_part = None
        return (row_total + jnp.sum(weights, axis=1), column_part)

    row_sums, column_sums = lax.scan(
        one_block, jnp.zeros((left_rows.shape[0],), jnp.float32), (right_blocks, id_blocks)
    )
    return (row_sums, column_sums)


def local(embeddings, cluster_ids, owner_map, source_order):
    row_count, feature_width = embeddings.shape
    owner_count = lax.axis_size("own")
    capacity = 2 * row_count // owner_count
    slot_count = owner_count * capacity
    cluster_count = owner_map.shape[0]
    unit_embed = unit_rows(embeddings)
    cluster_index = jnp.arange(cluster_count, dtype=jnp.int32)
    cluster_match = cluster_ids[:, None] == cluster_index[None, :]
    row_owner = jnp.sum(jnp.where(cluster_match, owner_map[None, :], 0), axis=1)
    owner_hot = (row_owner[:, None] == jnp.arange(owner_count, dtype=jnp.int32)[None, :]).astype(
        jnp.int32
    )
    rank_index = jnp.sum(jnp.cumsum(owner_hot, axis=0) * owner_hot, axis=1) - 1
    slot_index = row_owner * capacity + rank_index
    send_rows = jnp.zeros((slot_count, feature_width), jnp.float32).at[slot_index].set(unit_embed)
    send_ids = jnp.full((slot_count,), -1, jnp.int32).at[slot_index].set(cluster_ids)
    held_rows, held_ids = (
        lax.all_to_all(
            send_rows.reshape(owner_count, capacity, feature_width),
            "own",
            split_axis=0,
            concat_axis=0,
            tiled=True,
        ),
        lax.all_to_all(
            send_ids.reshape(owner_count, capacity), "own", split_axis=0, concat_axis=0, tiled=True
        ),
    )
    held_rows = held_rows.reshape(slot_count, feature_width)
    held_ids = held_ids.reshape(slot_count)
    row_sums, column_sums = tile_sums(
        held_rows,
        held_ids,
        lax.all_gather(held_rows, "grp", axis=0, tiled=True),
        lax.all_gather(held_ids, "grp", axis=0, tiled=True),
    )
    returned = lax.all_to_all(
        row_sums.reshape(owner_count, capacity), "own", split_axis=0, concat_axis=0, tiled=True
    )
    row_score = jnp.log(returned.reshape(slot_count)[slot_index])
    dup_score = jnp.zeros((row_count,), jnp.float32).at[source_order].set(row_score)
    position = owner_positions(owner_map)
    position_index = jnp.arange(cluster_count, dtype=jnp.int32)
    ordered = jnp.sum(
        jnp.where(position[None, :] == position_index[:, None], cluster_index[None, :], 0), axis=1
    )
    cluster_hot = (cluster_ids[:, None] == ordered[None, :]).astype(jnp.float32)
    cluster_terms = lax.dot_general(
        cluster_hot,
        unit_embed,
        (((0,), (0,)), ((), ())),
        preferred_element_type=jnp.float32,
        precision=lax.Precision.HIGHEST,
    )
    partial_value = lax.psum_scatter(cluster_terms, "own", scatter_dimension=0, tiled=True)
    cluster_sums = lax.psum(partial_value, "grp")
    centroids = cluster_sums * lax.rsqrt(
        jnp.mean(cluster_sums * cluster_sums, axis=1, keepdims=True) + 1e-06
    )
    return (dup_score, centroids)


def solution(mesh):
    placed = (P(("grp", "own"), None), P(("grp", "own")), P(), P(("grp", "own")))
    return jax.shard_map(
        local,
        mesh=mesh,
        in_specs=placed,
        out_specs=(P(("grp", "own")), P("own", None)),
        check_vma=False,
    )
```

profile of v0, /device:TPU:1, one launch (start us, length us, event | category | flops | bytes accessed | tf_op | source)
XLA Modules:
  0.0 433.6 jit_solution(5770465693371880921)
XLA Ops:
  13.3 9.7 %scatter_custom_fusion.1 = f32[1536,768]{1,0:T(8,128)} fusion(s32[768]{0:T(1024)S(1)} %fusion.26, f32[]{:T(128)} %constant.55.clone.1, f32[768,768]{1,0:T(8,128)S(1)} %copy-done, f32[768]{0:T(1024)S(1)} %add_rsqrt_fusion), kind=kCustom, calls=%fused_computation.17 | custom fusion | flops 589824 | bytes 7081988 | tf_op jit(solution)/shard_map/scatter | solution.py:70
  23.1 9.6 %all-to-all-start.1 = ((f32[32,48,768]{2,1,0:T(8,128)}), f32[32,48,768]{2,1,0:T(8,128)}, u32[]{:S(2)}, u32[]{:S(2)}) async-start(f32[32,48,768]{2,1,0:T(8,128)} %bitcast.46), calls=%async_computation.1 | async-start | bytes 9437184 | tf_op jit(solution)/shard_map/all_to_all | solution.py:73
  37.1 55.2 %all-to-all-done.1 = f32[32,48,768]{2,1,0:T(8,128)} async-done(((f32[32,48,768]{2,1,0:T(8,128)}), f32[32,48,768]{2,1,0:T(8,128)}, u32[]{:S(2)}, u32[]{:S(2)}) %all-to-all-start.1) | async-done | bytes 4718624 | tf_op jit(solution)/shard_map/all_to_all | solution.py:73
  96.4 9.8 %all-to-all-start = ((s32[32,1,48]{2,1,0:T(1,128)}), s32[32,1,48]{2,1,0:T(1,128)S(1)}, u32[]{:S(2)}, u32[]{:S(2)}) async-start(s32[32,1,48]{2,1,0:T(1,128)} %all_to_all.17), calls=%async_computation | async-start | bytes 32768 | tf_op jit(solution)/shard_map/all_to_all | solution.py:80
  106.2 6.8 %all-to-all-done = s32[32,1,48]{2,1,0:T(1,128)S(1)} async-done(((s32[32,1,48]{2,1,0:T(1,128)}), s32[32,1,48]{2,1,0:T(1,128)S(1)}, u32[]{:S(2)}, u32[]{:S(2)}) %all-to-all-start) | async-done | bytes 6176 | tf_op jit(solution)/shard_map/all_to_all | solution.py:80
  114.4 10.7 %all-gather = s32[4,1,1536]{2,1,0:T(1,128)S(1)} all-gather(s32[1,1,1536]{2,1,0:T(1,128)S(1)} %reshape.149), channel_id=1, replica_groups=mesh['grp'=4,'own'=32] {'grp'}, dimensions={0}, use_global_device_ids=true | all-gather | bytes 30720 | tf_op jit(solution)/shard_map/all_gather | solution.py:90
  125.1 16.3 %psum.7 = f32[16,768]{1,0:T(8,128)S(1)} all-reduce(f32[16,768]{1,0:T(8,128)} %reduce-scatter.2.cloned.1.call-done), channel_id=1, replica_groups=mesh['grp'=4,'own'=32] {'grp'}, use_global_device_ids=true, to_apply=%region_14.15 | all-reduce | flops 12288 | bytes 98304 | tf_op jit(solution)/shard_map/psum | solution.py:111
  141.6 127.8 %all-gather.3.cloned.1.call-done = f32[6144,768]{1,0:T(8,128)} async-done(((f32[1536,768]{1,0:T(8,128)}), f32[6144,768]{1,0:T(8,128)}) %all-gather.3.cloned.1.call-update) | async-done | bytes 18874384 | tf_op jit(solution)/shard_map/all_gather | solution.py:89
  269.4 131.6 %while.14 = (s32[]{:T(128)}, f32[1536]{0:T(1024)S(1)}, s32[32,48]{1,0:T(8,128)}, s32[12,512]{1,0:T(8,128)S(1)}, f32[12,512,768]{2,1,0:T(8,128)}, /*index=5*/f32[...) while((s32[]{:T(128)}, f32[1536]{0:T(1024)S(1)}, s32[32,48]{1,0:T(8,128)}, ...), condition=%wide.wide.region_9.10_spmd.clone, body=%wide.wide.region_7.9_spmd.clone.sunk | while | flops 7252478976 | bytes 6338155 | solution.py:49
  269.4 10.9 %fusion.38 = f32[1536]{0:T(1024)S(1)} fusion(f32[1536,768]{1,0:T(8,128)} %get-tuple-element.203, f32[12,512,768]{2,1,0:T(8,128)} %get-tuple-element.202, s32[]{:T(128)} %get-tuple-element.189, pred[1536]{0:T(1024)(128)(4,1)S(1)} %broadcast_compare_fusion.3, s32[512]{0:T(512)S(1)} %bitcast.50, s32[1536]{0:T(1024)S(1)} %get-tuple-element.204), kind=kOutput, calls=%fused_computation.11.clone.clone.1 | convolution fusion | flops 7252474368 | bytes 6307840 | tf_op jit(solution)/shard_map/while/body/eval_jaxpr/id,jd->ij/dot_general | solution.py:26
  280.4 10.9 %fusion.38 = f32[1536]{0:T(1024)S(1)} fusion(f32[1536,768]{1,0:T(8,128)} %get-tuple-element.203, f32[12,512,768]{2,1,0:T(8,128)} %get-tuple-element.202, s32[]{:T(128)} %get-tuple-element.189, pred[1536]{0:T(1024)(128)(4,1)S(1)} %broadcast_compare_fusion.3, s32[512]{0:T(512)S(1)} %bitcast.50, s32[1536]{0:T(1024)S(1)} %get-tuple-element.204), kind=kOutput, calls=%fused_computation.11.clone.clone.1 | convolution fusion | flops 7252474368 | bytes 6307840 | tf_op jit(solution)/shard_map/while/body/eval_jaxpr/id,jd->ij/dot_general | solution.py:26
  291.4 10.9 %fusion.38 = f32[1536]{0:T(1024)S(1)} fusion(f32[1536,768]{1,0:T(8,128)} %get-tuple-element.203, f32[12,512,768]{2,1,0:T(8,128)} %get-tuple-element.202, s32[]{:T(128)} %get-tuple-element.189, pred[1536]{0:T(1024)(128)(4,1)S(1)} %broadcast_compare_fusion.3, s32[512]{0:T(512)S(1)} %bitcast.50, s32[1536]{0:T(1024)S(1)} %get-tuple-element.204), kind=kOutput, calls=%fused_computation.11.clone.clone.1 | convolution fusion | flops 7252474368 | bytes 6307840 | tf_op jit(solution)/shard_map/while/body/eval_jaxpr/id,jd->ij/dot_general | solution.py:26
  302.3 10.9 %fusion.38 = f32[1536]{0:T(1024)S(1)} fusion(f32[1536,768]{1,0:T(8,128)} %get-tuple-element.203, f32[12,512,768]{2,1,0:T(8,128)} %get-tuple-element.202, s32[]{:T(128)} %get-tuple-element.189, pred[1536]{0:T(1024)(128)(4,1)S(1)} %broadcast_compare_fusion.3, s32[512]{0:T(512)S(1)} %bitcast.50, s32[1536]{0:T(1024)S(1)} %get-tuple-element.204), kind=kOutput, calls=%fused_computation.11.clone.clone.1 | convolution fusion | flops 7252474368 | bytes 6307840 | tf_op jit(solution)/shard_map/while/body/eval_jaxpr/id,jd->ij/dot_general | solution.py:26
  313.3 10.9 %fusion.38 = f32[1536]{0:T(1024)S(1)} fusion(f32[1536,768]{1,0:T(8,128)} %get-tuple-element.203, f32[12,512,768]{2,1,0:T(8,128)} %get-tuple-element.202, s32[]{:T(128)} %get-tuple-element.189, pred[1536]{0:T(1024)(128)(4,1)S(1)} %broadcast_compare_fusion.3, s32[512]{0:T(512)S(1)} %bitcast.50, s32[1536]{0:T(1024)S(1)} %get-tuple-element.204), kind=kOutput, calls=%fused_computation.11.clone.clone.1 | convolution fusion | flops 7252474368 | bytes 6307840 | tf_op jit(solution)/shard_map/while/body/eval_jaxpr/id,jd->ij/dot_general | solution.py:26
  324.3 10.9 %fusion.38 = f32[1536]{0:T(1024)S(1)} fusion(f32[1536,768]{1,0:T(8,128)} %get-tuple-element.203, f32[12,512,768]{2,1,0:T(8,128)} %get-tuple-element.202, s32[]{:T(128)} %get-tuple-element.189, pred[1536]{0:T(1024)(128)(4,1)S(1)} %broadcast_compare_fusion.3, s32[512]{0:T(512)S(1)} %bitcast.50, s32[1536]{0:T(1024)S(1)} %get-tuple-element.204), kind=kOutput, calls=%fused_computation.11.clone.clone.1 | convolution fusion | flops 7252474368 | bytes 6307840 | tf_op jit(solution)/shard_map/while/body/eval_jaxpr/id,jd->ij/dot_general | solution.py:26
  335.3 10.9 %fusion.38 = f32[1536]{0:T(1024)S(1)} fusion(f32[1536,768]{1,0:T(8,128)} %get-tuple-element.203, f32[12,512,768]{2,1,0:T(8,128)} %get-tuple-element.202, s32[]{:T(128)} %get-tuple-element.189, pred[1536]{0:T(1024)(128)(4,1)S(1)} %broadcast_compare_fusion.3, s32[512]{0:T(512)S(1)} %bitcast.50, s32[1536]{0:T(1024)S(1)} %get-tuple-element.204), kind=kOutput, calls=%fused_computation.11.clone.clone.1 | convolution fusion | flops 7252474368 | bytes 6307840 | tf_op jit(solution)/shard_map/while/body/eval_jaxpr/id,jd->ij/dot_general | solution.py:26
  346.2 10.9 %fusion.38 = f32[1536]{0:T(1024)S(1)} fusion(f32[1536,768]{1,0:T(8,128)} %get-tuple-element.203, f32[12,512,768]{2,1,0:T(8,128)} %get-tuple-element.202, s32[]{:T(128)} %get-tuple-element.189, pred[1536]{0:T(1024)(128)(4,1)S(1)} %broadcast_compare_fusion.3, s32[512]{0:T(512)S(1)} %bitcast.50, s32[1536]{0:T(1024)S(1)} %get-tuple-element.204), kind=kOutput, calls=%fused_computation.11.clone.clone.1 | convolution fusion | flops 7252474368 | bytes 6307840 | tf_op jit(solution)/shard_map/while/body/eval_jaxpr/id,jd->ij/dot_general | solution.py:26
  357.2 10.9 %fusion.38 = f32[1536]{0:T(1024)S(1)} fusion(f32[1536,768]{1,0:T(8,128)} %get-tuple-element.203, f32[12,512,768]{2,1,0:T(8,128)} %get-tuple-element.202, s32[]{:T(128)} %get-tuple-element.189, pred[1536]{0:T(1024)(128)(4,1)S(1)} %broadcast_compare_fusion.3, s32[512]{0:T(512)S(1)} %bitcast.50, s32[1536]{0:T(1024)S(1)} %get-tuple-element.204), kind=kOutput, calls=%fused_computation.11.clone.clone.1 | convolution fusion | flops 7252474368 | bytes 6307840 | tf_op jit(solution)/shard_map/while/body/eval_jaxpr/id,jd->ij/dot_general | solution.py:26
  368.2 10.9 %fusion.38 = f32[1536]{0:T(1024)S(1)} fusion(f32[1536,768]{1,0:T(8,128)} %get-tuple-element.203, f32[12,512,768]{2,1,0:T(8,128)} %get-tuple-element.202, s32[]{:T(128)} %get-tuple-element.189, pred[1536]{0:T(1024)(128)(4,1)S(1)} %broadcast_compare_fusion.3, s32[512]{0:T(512)S(1)} %bitcast.50, s32[1536]{0:T(1024)S(1)} %get-tuple-element.204), kind=kOutput, calls=%fused_computation.11.clone.clone.1 | convolution fusion | flops 7252474368 | bytes 6307840 | tf_op jit(solution)/shard_map/while/body/eval_jaxpr/id,jd->ij/dot_general | solution.py:26
  379.1 10.9 %fusion.38 = f32[1536]{0:T(1024)S(1)} fusion(f32[1536,768]{1,0:T(8,128)} %get-tuple-element.203, f32[12,512,768]{2,1,0:T(8,128)} %get-tuple-element.202, s32[]{:T(128)} %get-tuple-element.189, pred[1536]{0:T(1024)(128)(4,1)S(1)} %broadcast_compare_fusion.3, s32[512]{0:T(512)S(1)} %bitcast.50, s32[1536]{0:T(1024)S(1)} %get-tuple-element.204), kind=kOutput, calls=%fused_computation.11.clone.clone.1 | convolution fusion | flops 7252474368 | bytes 6307840 | tf_op jit(solution)/shard_map/while/body/eval_jaxpr/id,jd->ij/dot_general | solution.py:26
  390.1 10.9 %fusion.38 = f32[1536]{0:T(1024)S(1)} fusion(f32[1536,768]{1,0:T(8,128)} %get-tuple-element.203, f32[12,512,768]{2,1,0:T(8,128)} %get-tuple-element.202, s32[]{:T(128)} %get-tuple-element.189, pred[1536]{0:T(1024)(128)(4,1)S(1)} %broadcast_compare_fusion.3, s32[512]{0:T(512)S(1)} %bitcast.50, s32[1536]{0:T(1024)S(1)} %get-tuple-element.204), kind=kOutput, calls=%fused_computation.11.clone.clone.1 | convolution fusion | flops 7252474368 | bytes 6307840 | tf_op jit(solution)/shard_map/while/body/eval_jaxpr/id,jd->ij/dot_general | solution.py:26
  401.7 7.7 %all-to-all-start.2 = ((f32[32,1,48]{2,1,0:T(1,128)}), f32[32,1,48]{2,1,0:T(1,128)S(1)}, u32[]{:S(2)}, u32[]{:S(2)}) async-start(f32[32,1,48]{2,1,0:T(1,128)} %all_to_all.21), calls=%async_computation.2 | async-start | bytes 32768 | tf_op jit(solution)/shard_map/all_to_all | solution.py:92
  410.2 6.2 %all-to-all-done.2 = f32[32,1,48]{2,1,0:T(1,128)S(1)} async-done(((f32[32,1,48]{2,1,0:T(1,128)}), f32[32,1,48]{2,1,0:T(1,128)S(1)}, u32[]{:S(2)}, u32[]{:S(2)}) %all-to-all-start.2) | async-done | bytes 6176 | tf_op jit(solution)/shard_map/all_to_all | solution.py:92
  417.7 4.5 %gather_fusion = f32[768]{0:T(1024)S(1)} fusion(f32[1536]{0:T(1024)S(1)} %reshape.115, s32[1024]{0:T(1024)S(1)} %pad_clamp_fusion), kind=kCustom, calls=%fused_computation | custom fusion | bytes 9216 | tf_op jit(solution)/shard_map/gather | solution.py:95
  (85 shorter events, 22.1 us)
Async XLA Ops:
  8.0 5.3 %copy-start = (f32[768,768]{1,0:T(8,128)S(1)}, f32[768,768]{1,0:T(8,128)}, u32[]{:S(2)}) copy-start(f32[768,768]{1,0:T(8,128)} %param.6) | copy-start | bytes 7077892
  23.1 9.7 %copy-start.2 = (s32[512]{0:T(512)S(1)}, s32[512]{0:T(512)}, u32[]{:S(2)}) copy-start(s32[512]{0:T(512)} %param.8) | copy-start | bytes 6148
  23.1 10.1 %copy-start.3 = (s32[768]{0:T(1024)S(1)}, s32[768]{0:T(1024)}, u32[]{:S(2)}) copy-start(s32[768]{0:T(1024)} %param.7) | copy-start | bytes 9220
  23.1 69.2 %all-to-all-start.1 = ((f32[32,48,768]{2,1,0:T(8,128)}), f32[32,48,768]{2,1,0:T(8,128)}, u32[]{:S(2)}, u32[]{:S(2)}) async-start(f32[32,48,768]{2,1,0:T(8,128)} %bitcast.46), calls=%async_computation.1 | async-start | bytes 9437184 | tf_op jit(solution)/shard_map/all_to_all | solution.py:73
  32.7 92.4 %reduce-scatter.2.cloned.1.call-start = ((), (), s32[]{:S(2)}) async-start(), calls=%async_computation.5 | async-start | bytes 1622016 | tf_op jit(solution)/shard_map/reduce_scatter | solution.py:110
  37.0 232.4 %all-gather.3.cloned.1.call-start = ((), (), s32[]{:S(2)}) async-start(), calls=%async_computation.4 | async-start | bytes 23592960 | tf_op jit(solution)/shard_map/all_gather | solution.py:89
  92.3 13.9 %copy-start.4 = (s32[768]{0:T(1024)S(1)}, s32[768]{0:T(1024)}, u32[]{:S(2)}) copy-start(s32[768]{0:T(1024)} %param.9) | copy-start | bytes 9220
  96.4 16.6 %all-to-all-start = ((s32[32,1,48]{2,1,0:T(1,128)}), s32[32,1,48]{2,1,0:T(1,128)S(1)}, u32[]{:S(2)}, u32[]{:S(2)}) async-start(s32[32,1,48]{2,1,0:T(1,128)} %all_to_all.17), calls=%async_computation | async-start | bytes 32768 | tf_op jit(solution)/shard_map/all_to_all | solution.py:80
  113.1 156.3 %copy-start.1 = (s32[32,1,48]{2,1,0:T(1,128)}, s32[32,1,48]{2,1,0:T(1,128)S(1)}, u32[]{:S(2)}) copy-start(s32[32,1,48]{2,1,0:T(1,128)S(1)} %all-to-all-done) | copy-start | bytes 18436
  401.7 14.7 %all-to-all-start.2 = ((f32[32,1,48]{2,1,0:T(1,128)}), f32[32,1,48]{2,1,0:T(1,128)S(1)}, u32[]{:S(2)}, u32[]{:S(2)}) async-start(f32[32,1,48]{2,1,0:T(1,128)} %all_to_all.21), calls=%async_computation.2 | async-start | bytes 32768 | tf_op jit(solution)/shard_map/all_to_all | solution.py:92
Sparse Core Ops, SparseCore 0:
  37.1 80.2 reduce-scatter.1
Sparse Core Ops, SparseCore 1:
  92.4 176.9 all-gather.2
where the time goes:
time: 434 us
  waiting for transfers between devices  196 us (45%)
  matrix products  135 us (31%)
  starting transfers between devices  27.2 us (6%)
  blocking collectives  27 us (6%)
  other arithmetic  17.5 us (4%)
  between operations  15.7 us (4%)
  local copies, waits for them, and re-layouts  14.8 us (3%)
    dot_general x12, matrix products, masked_weights(): jnp.einsum('id,jd->ij', left_rows, right_rows, preferred_element_type=jnp...  131 us
    all_gather x1, waiting for transfers between devices, local(): lax.all_gather(held_rows, 'grp', axis=0, tiled=True)  128 us
    all_to_all x1, waiting for transfers between devices, local(): lax.all_to_all(send_rows.reshape(owner_count, capacity, feature_width), '...  55.2 us
    psum x1, blocking collectives, local(): cluster_sums = lax.psum(partial_value, 'grp')  16.3 us
    all_gather x1, blocking collectives, local(): lax.all_gather(held_ids, 'grp', axis=0, tiled=True)  10.7 us
    all_to_all x1, starting transfers between devices, local(): lax.all_to_all(send_ids.reshape(owner_count, capacity), 'own', split_axis...  9.77 us
    scatter x1, other arithmetic, local(): jnp.zeros((slot_count, feature_width), jnp.float32).at[slot_index]  9.72 us
    all_to_all x1, starting transfers between devices, local(): lax.all_to_all(send_rows.reshape(owner_count, capacity, feature_width), '...  9.61 us
  transfers between devices with their start and end apart: 5, of which 4 were waited for; matrix products, arithmetic and copies ran while one was open for 2% of the time, Pallas kernels for 0%

commit v1 on v0

v1 whole, which is shorter than its diff:
```python
import functools

import jax
import jax.numpy as jnp
from jax import lax
from jax.experimental import pallas as pl
from jax.experimental.pallas import tpu as pltpu
from jax.sharding import PartitionSpec as P

MESH = pl.DeviceIdType.MESH
F32 = jnp.float32
BF16 = jnp.bfloat16

N_GRP = 4
N_OWN = 32
D = 768
R_DEV = 768
CLUSTERS = 512
CL_OWN = 16
CAP = 48
SLOTS = N_OWN * CAP
MSGS = N_GRP * N_OWN
STEP = 13
CHUNK_MSGS = 16
CHUNK = CHUNK_MSGS * CAP
CHUNKS = MSGS // CHUNK_MSGS
SHARPNESS = 6.0


def hot(condition):
    return jnp.where(condition, 1.0, 0.0).astype(BF16)


def iota(shape, dim):
    return lax.broadcasted_iota(jnp.int32, shape, dim)


def by_48(n):
    return (n * 1366) >> 16


def dot(a, b):
    return lax.dot_general(a, b, (((1,), (0,)), ((), ())), preferred_element_type=F32)


def dot_t(a, b):
    return lax.dot_general(a, b, (((1,), (1,)), ((), ())), preferred_element_type=F32)


def split3(a):
    high = a.astype(BF16)
    rest = a - high.astype(F32)
    middle = rest.astype(BF16)
    low = (rest - middle.astype(F32)).astype(BF16)
    return high, middle, low


def exact(product, a, b):
    high, middle, low = split3(a)
    return product(high, b) + (product(middle, b) + product(low, b))


def home_row(owner):
    x, z, core = owner // 8, lax.rem(owner // 2, 4), lax.rem(owner, 2)
    return lax.rem(x + z, 2) + 2 * core


def kernel(
    x_ref, cid_ref, map_ref, order_ref, dup_ref, cen_ref,
    packed, ids_out, land, ids_in, unit, row_acc, col_acc, id_col, id_row, sums, rowhot_ref, rank_ref,
    mass_out, mass_in, cen_in,
    send_sem, ids_send_sem, recv_sem, ids_recv_sem, local_sem, back_send_sem, back_recv_sem, cen_send_sem, cen_recv_sem,
):
    me, grp = lax.axis_index("own"), lax.axis_index("grp")
    home = grp == home_row(me)

    owner_hot = hot(iota((N_OWN, CLUSTERS), 0) == map_ref[...])
    earlier = hot(iota((CLUSTERS, CLUSTERS), 0) < iota((CLUSTERS, CLUSTERS), 1))
    before = dot(owner_hot, earlier)
    place = jnp.sum(owner_hot.astype(F32) * before, axis=0, keepdims=True)
    table = jnp.concatenate([owner_hot, jnp.broadcast_to(place, (16, CLUSTERS)).astype(BF16)], axis=0)
    looked_up = dot(table, hot(iota((CLUSTERS, R_DEV), 0) == cid_ref[...]))
    row_hot, row_place = looked_up[:N_OWN], looked_up[N_OWN : N_OWN + 1]
    ahead = hot(iota((R_DEV, R_DEV), 0) < iota((R_DEV, R_DEV), 1))
    rank = jnp.sum(row_hot * dot(row_hot.astype(BF16), ahead), axis=0, keepdims=True)
    owner = jnp.sum(row_hot * iota((N_OWN, R_DEV), 0).astype(F32), axis=0, keepdims=True)
    rank = rank.astype(jnp.int32)
    slot = owner.astype(jnp.int32) * CAP + rank
    rank_hot = hot(iota((128, R_DEV), 0) == rank)
    rowhot_ref[...] = row_hot
    rank_ref[...] = rank_hot
    ids = dot_t((row_hot * (row_place + 1.0)).astype(BF16), rank_hot) - 1.0
    for o in range(N_OWN):
        ids_out[o] = jnp.broadcast_to(ids[o : o + 1], (8, 128))

    x = x_ref[...]
    u = x * lax.rsqrt(jnp.sum(x * x, axis=1, keepdims=True) + 1e-06)
    high = u.astype(BF16)
    low = (u - high.astype(F32)).astype(BF16)
    block = SLOTS // 4
    for k in range(4):
        pick = hot(iota((block, R_DEV), 0) + k * block == slot)
        packed[pl.ds(k * block, block)] = dot(pick, high) + dot(pick, low)

    def send(i, _):
        o = lax.rem(me + lax.rem(STEP * i, N_OWN), N_OWN)
        to = home_row(o)
        here = (o == me) & (to == grp)
        start = pl.multiple_of(o * CAP, CAP)
        m = i * N_GRP + grp
        stop = pl.multiple_of(m * CAP, CAP)

        @pl.when(jnp.logical_not(here))
        def _():
            pltpu.make_async_remote_copy(
                src_ref=ids_out.at[o], dst_ref=ids_in.at[m], send_sem=ids_send_sem,
                recv_sem=ids_recv_sem.at[i // N_GRP], device_id=(to, o), device_id_type=MESH,
            ).start()
            pltpu.make_async_remote_copy(
                src_ref=packed.at[pl.ds(start, CAP)], dst_ref=land.at[pl.ds(stop, CAP)], send_sem=send_sem,
                recv_sem=recv_sem.at[i // N_GRP], device_id=(to, o), device_id_type=MESH,
            ).start()

        @pl.when(here)
        def _():
            pltpu.make_async_copy(ids_out.at[o], ids_in.at[m], local_sem.at[0]).start()
            pltpu.make_async_copy(packed.at[pl.ds(start, CAP)], land.at[pl.ds(stop, CAP)], local_sem.at[1]).start()

        return 0

    lax.fori_loop(0, N_OWN, send, 0)

    def wait(ref, count, sem):
        pltpu.make_async_copy(ref.at[pl.ds(0, count)], ref.at[pl.ds(0, count)], sem).wait()

    cols = iota((128, CHUNK), 1)
    spread = hot(cols - CAP * by_48(cols) == iota((128, CHUNK), 0))
    mine = by_48(iota((CHUNK_MSGS, CHUNK), 1)) == iota((CHUNK_MSGS, CHUNK), 0)

    def pair(a, b, diagonal):
        left = pl.multiple_of(a * CHUNK, CHUNK)
        right = pl.multiple_of(b * CHUNK, CHUNK)
        part = 256
        cols_sum = [jnp.zeros((8, 128), F32)] * (CHUNK // 128)
        for r in range(CHUNK // part):
            rows = pl.ds(left + r * part, part)
            scores = dot_t(unit[rows], unit[pl.ds(right, CHUNK)])
            left_ids = id_col[rows]
            total = row_acc[rows]
            for t in range(CHUNK // 128):
                weights = jnp.exp(SHARPNESS * scores[:, t * 128 : (t + 1) * 128] - SHARPNESS)
                same = left_ids == id_row[0:1, pl.ds(right + t * 128, 128)]
                weights = jnp.where(same, weights, 0.0)
                total = total + weights
                if not diagonal:
                    cols_sum[t] = cols_sum[t] + jnp.sum(weights.reshape(part // 8, 8, 128), axis=0)
            row_acc[rows] = total
        if not diagonal:
            for t in range(CHUNK // 128):
                col_acc[:, pl.ds(right + t * 128, 128)] += cols_sum[t]

    @pl.when(home)
    def _():
        sums[...] = jnp.zeros_like(sums)
        row_acc[...] = jnp.zeros_like(row_acc)
        col_acc[...] = jnp.zeros_like(col_acc)
        wait(ids_out, 1, local_sem.at[0])
        pltpu.make_async_copy(packed.at[pl.ds(0, CAP)], packed.at[pl.ds(0, CAP)], local_sem.at[1]).wait()

        def chunk(a, _):
            @pl.when(a == 0)
            def _():
                wait(ids_in, CHUNK_MSGS - 1, ids_recv_sem.at[0])
                wait(land, CHUNK - CAP, recv_sem.at[0])

            @pl.when(a > 0)
            def _():
                wait(ids_in, CHUNK_MSGS, ids_recv_sem.at[a])
                wait(land, CHUNK, recv_sem.at[a])

            base = pl.multiple_of(a * CHUNK, CHUNK)
            rows = pl.ds(base, CHUNK)
            got = land[rows]
            high = got.astype(BF16)
            unit[rows] = high
            low = (got - high.astype(F32)).astype(BF16)
            ids = ids_in[pl.ds(a * CHUNK_MSGS, CHUNK_MSGS), 0, :].astype(BF16)
            in_row = jnp.where(mine, dot(ids, spread), 0.0).astype(BF16)
            row = dot(jnp.ones((8, CHUNK_MSGS), BF16), in_row)
            id_row[:, rows] = row
            at = iota((CHUNK, 128), 0)
            picked = dot(hot(by_48(iota((CHUNK, CHUNK_MSGS), 0)) == iota((CHUNK, CHUNK_MSGS), 1)), ids)
            picked = jnp.where(at - CAP * by_48(at) == iota((CHUNK, 128), 1), picked, 0.0).astype(BF16)
            id_col[rows] = dot(picked, jnp.ones((128, 128), BF16))
            member = hot(iota((CL_OWN, CHUNK), 0).astype(F32) == row[0:1])
            sums[...] += dot(member, high) + dot(member, low)
            lax.fori_loop(0, a, lambda b, _: (pair(a, b, False), 0)[1], 0)
            pair(a, a, True)
            return 0

        lax.fori_loop(0, CHUNKS, chunk, 0)

        def give_back(a, _):
            rows = pl.ds(pl.multiple_of(a * CHUNK, CHUNK), CHUNK)
            part = row_acc[rows]
            high, middle, low = split3(part)
            ones = jnp.ones((8, 128), BF16)
            mass = dot_t(ones, high) + (dot_t(ones, middle) + dot_t(ones, low))
            mass = mass[0:1] + jnp.sum(col_acc[:, rows], axis=0, keepdims=True)
            back = exact(dot_t, jnp.where(mine, mass, 0.0), spread)
            for j in range(CHUNK_MSGS):
                mass_out[a * CHUNK_MSGS + j] = jnp.broadcast_to(back[j : j + 1], (8, 128))
            for j in range(CHUNK_MSGS):
                i = a * (CHUNK_MSGS // N_GRP) + j // N_GRP
                to_grp = j % N_GRP
                to = lax.rem(me + N_OWN - lax.rem(STEP * i, N_OWN), N_OWN)
                here = (to == me) & (grp == to_grp)

                @pl.when(jnp.logical_not(here))
                def _():
                    pltpu.make_async_remote_copy(
                        src_ref=mass_out.at[a * CHUNK_MSGS + j], dst_ref=mass_in.at[me], send_sem=back_send_sem,
                        recv_sem=back_recv_sem, device_id=(to_grp, to), device_id_type=MESH,
                    ).start()

                @pl.when(here)
                def _():
                    pltpu.make_async_copy(mass_out.at[a * CHUNK_MSGS + j], mass_in.at[me], local_sem.at[2]).start()

            return 0

        lax.fori_loop(0, CHUNKS, give_back, 0)

        total = sums[...]
        cen_ref[...] = total * lax.rsqrt(jnp.mean(total * total, axis=1, keepdims=True) + 1e-06)
        for k in range(1, N_GRP):
            pltpu.make_async_remote_copy(
                src_ref=cen_ref, dst_ref=cen_in, send_sem=cen_send_sem.at[k - 1], recv_sem=cen_recv_sem,
                device_id=(lax.rem(grp + k, N_GRP), me), device_id_type=MESH,
            ).start()
        for k in range(1, N_GRP):
            pltpu.make_async_copy(cen_ref, cen_ref, cen_send_sem.at[k - 1]).wait()
        wait(mass_out, MSGS - 1, back_send_sem)
        wait(mass_out, 1, local_sem.at[2])
        wait(mass_in, N_OWN - 1, back_recv_sem)
        wait(packed, SLOTS - CAP, send_sem)
        wait(ids_out, N_OWN - 1, ids_send_sem)

    @pl.when(jnp.logical_not(home))
    def _():
        pltpu.make_async_copy(cen_in, cen_in, cen_recv_sem).wait()
        cen_ref[...] = cen_in[...]
        wait(mass_in, N_OWN, back_recv_sem)
        wait(packed, SLOTS, send_sem)
        wait(ids_out, N_OWN, ids_send_sem)

    got = exact(dot, mass_in[:, 0, :], rank_ref[...])
    mass = jnp.sum(got * rowhot_ref[...], axis=0, keepdims=True)
    score = jnp.broadcast_to(jnp.log(mass), (8, R_DEV))
    target = hot(iota((R_DEV, R_DEV), 0) == order_ref[...])
    dup_ref[...] = exact(dot_t, score, target)[0:1]


def local(embeddings, cluster_ids, owner_map, source_order):
    vmem = pl.BlockSpec(memory_space=pltpu.VMEM)
    dma = pltpu.SemaphoreType.DMA
    dup, centroids = pl.pallas_call(
        kernel,
        out_shape=(jax.ShapeDtypeStruct((1, R_DEV), F32), jax.ShapeDtypeStruct((CL_OWN, D), F32)),
        in_specs=[vmem] * 4,
        out_specs=(vmem, vmem),
        scratch_shapes=[
            pltpu.VMEM((SLOTS, D), F32),
            pltpu.VMEM((N_OWN, 8, 128), F32),
            pltpu.VMEM((MSGS * CAP, D), F32),
            pltpu.VMEM((MSGS, 8, 128), F32),
            pltpu.VMEM((MSGS * CAP, D), BF16),
            pltpu.VMEM((MSGS * CAP, 128), F32),
            pltpu.VMEM((8, MSGS * CAP), F32),
            pltpu.VMEM((MSGS * CAP, 128), F32),
            pltpu.VMEM((8, MSGS * CAP), F32),
            pltpu.VMEM((CL_OWN, D), F32),
            pltpu.VMEM((N_OWN, R_DEV), F32),
            pltpu.VMEM((128, R_DEV), BF16),
            pltpu.VMEM((MSGS, 8, 128), F32),
            pltpu.VMEM((N_OWN, 8, 128), F32),
            pltpu.VMEM((CL_OWN, D), F32),
            dma, dma, dma((CHUNKS,)), dma((CHUNKS,)), dma((3,)), dma, dma, dma((3,)), dma,
        ],
        compiler_params=pltpu.CompilerParams(has_side_effects=True, vmem_limit_bytes=60 << 20),
        name="owner_gather",
    )(
        embeddings,
        cluster_ids.reshape(1, R_DEV),
        owner_map.reshape(1, CLUSTERS),
        source_order.reshape(1, R_DEV),
    )
    return dup.reshape(R_DEV), centroids


def solution(mesh):
    placed = (P(("grp", "own"), None), P(("grp", "own")), P(), P(("grp", "own")))
    return jax.shard_map(
        local,
        mesh=mesh,
        in_specs=placed,
        out_specs=(P(("grp", "own")), P("own", None)),
        check_vma=False,
    )
```

time: 434 us -> 194 us (0.45)
  waiting for transfers between devices: 196 us -> 0 us
  Pallas kernels: 0 us -> 188 us
  matrix products: 135 us -> 0 us
  starting transfers between devices: 27.2 us -> 0 us
  blocking collectives: 27 us -> 0 us
  other arithmetic: 17.5 us -> 1.28 us
  between operations: 15.7 us -> 0.64 us
  local copies, waits for them, and re-layouts: 14.8 us -> 3.95 us
    pallas_call x0 -> x1, Pallas kernels: none -> 188 us  [local(): pl.pallas_call(kernel, out_shape=(jax.ShapeDtypeStruct((1, R_DEV), F32),...]
    dot_general x13 -> x0, matrix products: 135 us -> none  [the longest x12 131 us: masked_weights(): jnp.einsum('id,jd->ij', left_rows, right_rows, preferred_element_type=jnp...]
    all_gather x1 -> x0, waiting for transfers between devices: 128 us -> none  [local(): lax.all_gather(held_rows, 'grp', axis=0, tiled=True)]
    all_to_all x3 -> x0, waiting for transfers between devices: 68.3 us -> none  [the longest x1 55.2 us: local(): lax.all_to_all(send_rows.reshape(owner_count, capacity, feature_width), '...]
    all_to_all x3 -> x0, starting transfers between devices: 27.1 us -> none  [the longest x1 9.77 us: local(): lax.all_to_all(send_ids.reshape(owner_count, capacity), 'own', split_axis...]
    psum x1 -> x0, blocking collectives: 16.3 us -> none  [local(): cluster_sums = lax.psum(partial_value, 'grp')]
    all_gather x1 -> x0, blocking collectives: 10.7 us -> none  [local(): lax.all_gather(held_ids, 'grp', axis=0, tiled=True)]
    scatter x1 -> x0, other arithmetic: 9.72 us -> none  [local(): jnp.zeros((slot_count, feature_width), jnp.float32).at[slot_index]]
  transfers between devices with their start and end apart: 5 -> 0, of which waited for: 4 -> 0; matrix products, arithmetic and copies ran while one was open for 2% -> 0% of each run, Pallas kernels for 0% -> 0%
where the time goes in v1:
time: 194 us
  Pallas kernels  188 us (97%)
  local copies, waits for them, and re-layouts  3.95 us (2%)
    pallas_call x1, Pallas kernels, local(): pl.pallas_call(kernel, out_shape=(jax.ShapeDtypeStruct((1, R_DEV), F32),...  188 us

profile of v1, /device:TPU:1, one launch (start us, length us, event | category | flops | bytes accessed | tf_op | source)
XLA Modules:
  0.0 194.0 jit_solution(17486681678971208028)
XLA Ops:
  0.6 1.3 reshape.16.cid_ref
  1.9 1.3 reshape.18.order_ref
  3.2 188.2 %owner_gather.1 = (f32[1,768]{1,0:T(1,128)}, f32[16,768]{1,0:T(8,128)}) custom-call(f32[768,768]{1,0:T(8,128)} %x_ref.1, s32[1,768]{1,0:T(1,128)} %reshape.16.cid_ref, s32[1,512]{1,0:T(1,128)} %bitcast.1, s32[1,768]{1,0:T(1,128)} %reshape.18.order_ref), custom_call_target="tpu_custom_call" | custom-call | tf_op jit(solution)/shard_map/owner_gather/pallas_call | solution.py:267
  191.3 1.3 reduce
  192.6 1.4 copy.7

commit v2 on v1

--- a/solution.py
+++ b/solution.py
@@ -25,6 +25,8 @@
 CHUNK = CHUNK_MSGS * CAP
 CHUNKS = MSGS // CHUNK_MSGS
 SHARPNESS = 6.0
+WINDOW = 8
+LAG = 6
 
 
 def hot(condition):
@@ -65,11 +67,19 @@
     return lax.rem(x + z, 2) + 2 * core
 
 
+def in_transit(source, grp, owner):
+    z_step = lax.rem(owner // 2 - source // 2 + 2 * N_OWN, 4)
+    y_step = lax.rem(home_row(owner) - grp + 4, 4)
+    via = ((y_step == 1) & (z_step >= 2)) | ((y_step == 3) & (z_step >= 1) & (z_step <= 2))
+    late = jnp.where(y_step == 1, z_step - 2, z_step - 1)
+    return via, late * 8 + source // 8 * 2 + lax.rem(source, 2)
+
+
 def kernel(
     x_ref, cid_ref, map_ref, order_ref, dup_ref, cen_ref,
-    packed, ids_out, land, ids_in, unit, row_acc, col_acc, id_col, id_row, sums, rowhot_ref, rank_ref,
-    mass_out, mass_in, cen_in,
-    send_sem, ids_send_sem, recv_sem, ids_recv_sem, local_sem, back_send_sem, back_recv_sem, cen_send_sem, cen_recv_sem,
+    packed, ids_out, land, ids_in, unit, row_acc, col_acc, id_col, id_row, scale_col, scale_row, sums, rowhot_ref, rank_ref,
+    mass_out, mass_in, cen_in, transit,
+    send_sem, transit_sem, pass_sem, ids_send_sem, recv_sem, ids_recv_sem, local_sem, back_send_sem, back_recv_sem, cen_send_sem, cen_recv_sem,
 ):
     me, grp = lax.axis_index("own"), lax.axis_index("grp")
     home = grp == home_row(me)
@@ -102,13 +112,15 @@
         pick = hot(iota((block, R_DEV), 0) + k * block == slot)
         packed[pl.ds(k * block, block)] = dot(pick, high) + dot(pick, low)
 
-    def send(i, _):
+    def at_slot(m):
+        return pl.ds(pl.multiple_of(m * CAP, CAP), CAP)
+
+    def send(i):
         o = lax.rem(me + lax.rem(STEP * i, N_OWN), N_OWN)
         to = home_row(o)
         here = (o == me) & (to == grp)
-        start = pl.multiple_of(o * CAP, CAP)
+        via, place = in_transit(me, grp, o)
         m = i * N_GRP + grp
-        stop = pl.multiple_of(m * CAP, CAP)
 
         @pl.when(jnp.logical_not(here))
         def _():
@@ -116,19 +128,64 @@
                 src_ref=ids_out.at[o], dst_ref=ids_in.at[m], send_sem=ids_send_sem,
                 recv_sem=ids_recv_sem.at[i // N_GRP], device_id=(to, o), device_id_type=MESH,
             ).start()
-            pltpu.make_async_remote_copy(
-                src_ref=packed.at[pl.ds(start, CAP)], dst_ref=land.at[pl.ds(stop, CAP)], send_sem=send_sem,
+
+        @pl.when(jnp.logical_not(here | via))
+        def _():
+            pltpu.make_async_remote_copy(
+                src_ref=packed.at[at_slot(o)], dst_ref=land.at[at_slot(m)], send_sem=send_sem.at[i],
                 recv_sem=recv_sem.at[i // N_GRP], device_id=(to, o), device_id_type=MESH,
             ).start()
 
+        @pl.when(via)
+        def _():
+            pltpu.make_async_remote_copy(
+                src_ref=packed.at[at_slot(o)], dst_ref=transit.at[at_slot(place)], send_sem=send_sem.at[i],
+                recv_sem=transit_sem.at[i], device_id=(grp, o), device_id_type=MESH,
+            ).start()
+
         @pl.when(here)
         def _():
             pltpu.make_async_copy(ids_out.at[o], ids_in.at[m], local_sem.at[0]).start()
-            pltpu.make_async_copy(packed.at[pl.ds(start, CAP)], land.at[pl.ds(stop, CAP)], local_sem.at[1]).start()
-
-        return 0
-
-    lax.fori_loop(0, N_OWN, send, 0)
+            pltpu.make_async_copy(packed.at[at_slot(o)], land.at[at_slot(m)], send_sem.at[i]).start()
+
+    def pass_on(i):
+        source = lax.rem(me + N_OWN - lax.rem(STEP * i, N_OWN), N_OWN)
+        via, place = in_transit(source, grp, me)
+
+        @pl.when(via)
+        def _():
+            here = transit.at[at_slot(place)]
+            pltpu.make_async_copy(here, here, transit_sem.at[i]).wait()
+            pltpu.make_async_remote_copy(
+                src_ref=here, dst_ref=land.at[at_slot(i * N_GRP + grp)], send_sem=pass_sem,
+                recv_sem=recv_sem.at[i // N_GRP], device_id=(home_row(me), me), device_id_type=MESH,
+            ).start()
+
+    def sent(i):
+        pltpu.make_async_copy(packed.at[at_slot(0)], packed.at[at_slot(0)], send_sem.at[i]).wait()
+
+    @pl.when(home)
+    def _():
+        lax.fori_loop(0, N_OWN, lambda i, _: (send(i), 0)[1], 0)
+
+    @pl.when(jnp.logical_not(home))
+    def _():
+        def step(i, _):
+            @pl.when((i >= WINDOW) & (i < N_OWN + WINDOW))
+            def _():
+                sent(i - WINDOW)
+
+            @pl.when(i < N_OWN)
+            def _():
+                send(i)
+
+            @pl.when((i >= LAG) & (i < N_OWN + LAG))
+            def _():
+                pass_on(i - LAG)
+
+            return 0
+
+        lax.fori_loop(0, N_OWN + max(WINDOW, LAG), step, 0)
 
     def wait(ref, count, sem):
         pltpu.make_async_copy(ref.at[pl.ds(0, count)], ref.at[pl.ds(0, count)], sem).wait()
@@ -146,10 +203,13 @@
             rows = pl.ds(left + r * part, part)
             scores = dot_t(unit[rows], unit[pl.ds(right, CHUNK)])
             left_ids = id_col[rows]
+            left_scale = scale_col[rows]
             total = row_acc[rows]
             for t in range(CHUNK // 128):
-                weights = jnp.exp(SHARPNESS * scores[:, t * 128 : (t + 1) * 128] - SHARPNESS)
-                same = left_ids == id_row[0:1, pl.ds(right + t * 128, 128)]
+                lanes = pl.ds(right + t * 128, 128)
+                scaled = scores[:, t * 128 : (t + 1) * 128] * left_scale * scale_row[0:1, lanes]
+                weights = jnp.exp(scaled - SHARPNESS)
+                same = left_ids == id_row[0:1, lanes]
                 weights = jnp.where(same, weights, 0.0)
                 total = total + weights
                 if not diagonal:
@@ -165,7 +225,7 @@
         row_acc[...] = jnp.zeros_like(row_acc)
         col_acc[...] = jnp.zeros_like(col_acc)
         wait(ids_out, 1, local_sem.at[0])
-        pltpu.make_async_copy(packed.at[pl.ds(0, CAP)], packed.at[pl.ds(0, CAP)], local_sem.at[1]).wait()
+        sent(0)
 
         def chunk(a, _):
             @pl.when(a == 0)
@@ -183,7 +243,14 @@
             got = land[rows]
             high = got.astype(BF16)
             unit[rows] = high
-            low = (got - high.astype(F32)).astype(BF16)
+            wide = high.astype(F32)
+            low = (got - wide).astype(BF16)
+            kept = jnp.sum(wide * wide, axis=1, keepdims=True)
+            off = jnp.sqrt(jnp.sum(got * got, axis=1, keepdims=True) / jnp.maximum(kept, 1e-30))
+            off = jnp.where(kept > 0.0, off - 1.0, 0.0)
+            off = jnp.broadcast_to(off, (CHUNK, 128))
+            scale_col[rows] = SHARPNESS + SHARPNESS * off
+            scale_row[:, rows] = 1.0 + dot_t(hot(iota((8, 128), 1) == 0), off.astype(BF16))
             ids = ids_in[pl.ds(a * CHUNK_MSGS, CHUNK_MSGS), 0, :].astype(BF16)
             in_row = jnp.where(mine, dot(ids, spread), 0.0).astype(BF16)
             row = dot(jnp.ones((8, CHUNK_MSGS), BF16), in_row)
@@ -243,7 +310,7 @@
         wait(mass_out, MSGS - 1, back_send_sem)
         wait(mass_out, 1, local_sem.at[2])
         wait(mass_in, N_OWN - 1, back_recv_sem)
-        wait(packed, SLOTS - CAP, send_sem)
+        lax.fori_loop(1, N_OWN, lambda i, _: (sent(i), 0)[1], 0)
         wait(ids_out, N_OWN - 1, ids_send_sem)
 
     @pl.when(jnp.logical_not(home))
@@ -251,7 +318,11 @@
         pltpu.make_async_copy(cen_in, cen_in, cen_recv_sem).wait()
         cen_ref[...] = cen_in[...]
         wait(mass_in, N_OWN, back_recv_sem)
-        wait(packed, SLOTS, send_sem)
+
+        @pl.when(lax.rem(home_row(me) + grp, 2) == 1)
+        def _():
+            wait(transit, 16 * CAP, pass_sem)
+
         wait(ids_out, N_OWN, ids_send_sem)
 
     got = exact(dot, mass_in[:, 0, :], rank_ref[...])
@@ -279,13 +350,16 @@
             pltpu.VMEM((8, MSGS * CAP), F32),
             pltpu.VMEM((MSGS * CAP, 128), F32),
             pltpu.VMEM((8, MSGS * CAP), F32),
+            pltpu.VMEM((MSGS * CAP, 128), F32),
+            pltpu.VMEM((8, MSGS * CAP), F32),
             pltpu.VMEM((CL_OWN, D), F32),
             pltpu.VMEM((N_OWN, R_DEV), F32),
             pltpu.VMEM((128, R_DEV), BF16),
             pltpu.VMEM((MSGS, 8, 128), F32),
             pltpu.VMEM((N_OWN, 8, 128), F32),
             pltpu.VMEM((CL_OWN, D), F32),
-            dma, dma, dma((CHUNKS,)), dma((CHUNKS,)), dma((3,)), dma, dma, dma((3,)), dma,
+            pltpu.VMEM((16 * CAP, D), F32),
+            dma((N_OWN,)), dma((N_OWN,)), dma, dma, dma((CHUNKS,)), dma((CHUNKS,)), dma((3,)), dma, dma, dma((3,)), dma,
         ],
         compiler_params=pltpu.CompilerParams(has_side_effects=True, vmem_limit_bytes=60 << 20),
         name="owner_gather",

time: 194 us -> 153 us (0.79)
  Pallas kernels: 188 us -> 146 us
    pallas_call x1, Pallas kernels: 188 us -> 146 us  [local(): pl.pallas_call(kernel, out_shape=(jax.ShapeDtypeStruct((1, R_DEV), F32),...]
where the time goes in v2:
time: 153 us; the launch traced here: 152 us
  Pallas kernels  146 us (95%)
  local copies, waits for them, and re-layouts  3.95 us (3%)
    pallas_call x1, Pallas kernels, local(): pl.pallas_call(kernel, out_shape=(jax.ShapeDtypeStruct((1, R_DEV), F32),...  146 us

profile of v2, /device:TPU:1, one launch (start us, length us, event | category | flops | bytes accessed | tf_op | source)
XLA Modules:
  0.0 151.8 jit_solution(14729481175005948469)
XLA Ops:
  0.6 1.3 reshape.16.cid_ref
  1.9 1.3 reshape.18.order_ref
  3.2 146.0 %owner_gather.1 = (f32[1,768]{1,0:T(1,128)}, f32[16,768]{1,0:T(8,128)}) custom-call(f32[768,768]{1,0:T(8,128)} %x_ref.1, s32[1,768]{1,0:T(1,128)} %reshape.16.cid_ref, s32[1,512]{1,0:T(1,128)} %bitcast.1, s32[1,768]{1,0:T(1,128)} %reshape.18.order_ref), custom_call_target="tpu_custom_call" | custom-call | tf_op jit(solution)/shard_map/owner_gather/pallas_call | solution.py:338
  149.1 1.3 reduce
  150.4 1.4 copy.7

commit v3 on v2

--- a/solution.py
+++ b/solution.py
@@ -20,13 +20,14 @@
 CAP = 48
 SLOTS = N_OWN * CAP
 MSGS = N_GRP * N_OWN
-STEP = 13
 CHUNK_MSGS = 16
 CHUNK = CHUNK_MSGS * CAP
 CHUNKS = MSGS // CHUNK_MSGS
 SHARPNESS = 6.0
+SELF = 31
 WINDOW = 8
-LAG = 6
+PACKS = 4
+LAG = 3
 
 
 def hot(condition):
@@ -67,6 +68,25 @@
     return lax.rem(x + z, 2) + 2 * core
 
 
+def partner(me, i, back=False):
+    a, b, c = lax.rem(i, 4), lax.rem(i // 4, 4), i // 16
+    dx = lax.rem(10 - a - b, 4)
+    dz = jnp.where(a == 0, 2, jnp.where(a == 1, 1, jnp.where(a == 2, 3, 0)))
+    dc = lax.rem(a + c, 2)
+    if back:
+        dx, dz = 4 - dx, 4 - dz
+    x, z, core = me // 8, lax.rem(me // 2, 4), lax.rem(me, 2)
+    return lax.rem(x + dx, 4) * 8 + lax.rem(z + dz, 4) * 2 + lax.rem(core + dc, 2)
+
+
+def step_to(me, owner):
+    dx = lax.rem(owner // 8 - me // 8 + 8, 4)
+    dz = lax.rem(lax.rem(owner // 2, 4) - lax.rem(me // 2, 4) + 4, 4)
+    dc = lax.rem(owner + me, 2)
+    a = jnp.where(dz == 2, 0, jnp.where(dz == 1, 1, jnp.where(dz == 3, 2, 3)))
+    return a + 4 * lax.rem(18 - a - dx, 4) + 16 * lax.rem(dc + a, 2)
+
+
 def in_transit(source, grp, owner):
     z_step = lax.rem(owner // 2 - source // 2 + 2 * N_OWN, 4)
     y_step = lax.rem(home_row(owner) - grp + 4, 4)
@@ -78,45 +98,97 @@
 def kernel(
     x_ref, cid_ref, map_ref, order_ref, dup_ref, cen_ref,
     packed, ids_out, land, ids_in, unit, row_acc, col_acc, id_col, id_row, scale_col, scale_row, sums, rowhot_ref, rank_ref,
-    mass_out, mass_in, cen_in, transit,
+    mass_out, mass_in, cen_in, transit, x_held,
     send_sem, transit_sem, pass_sem, ids_send_sem, recv_sem, ids_recv_sem, local_sem, back_send_sem, back_recv_sem, cen_send_sem, cen_recv_sem,
 ):
     me, grp = lax.axis_index("own"), lax.axis_index("grp")
     home = grp == home_row(me)
 
-    owner_hot = hot(iota((N_OWN, CLUSTERS), 0) == map_ref[...])
+    barrier = pltpu.get_barrier_semaphore()
+
+    def tell(grp_to, own_to):
+        pl.semaphore_signal(barrier, inc=1, device_id=(grp_to, own_to), device_id_type=MESH)
+
+    def tell_home(o, _):
+        to = home_row(o)
+
+        @pl.when(jnp.logical_not(home & (o == me)))
+        def _():
+            tell(to, o)
+
+        return 0
+
+    lax.fori_loop(0, N_OWN, tell_home, 0)
+
+    @pl.when(home)
+    def _():
+        def tell_others(m, _):
+            @pl.when(home_row(m // N_GRP) != lax.rem(m, N_GRP))
+            def _():
+                tell(lax.rem(m, N_GRP), m // N_GRP)
+
+            return 0
+
+        lax.fori_loop(0, MSGS, tell_others, 0)
+
+    @pl.when(jnp.logical_not(home))
+    def _():
+        def tell_senders(o, _):
+            @pl.when(in_transit(o, grp, me)[0] & (home_row(o) != grp))
+            def _():
+                tell(grp, o)
+
+            return 0
+
+        lax.fori_loop(0, N_OWN, tell_senders, 0)
+
+    x_copy = pltpu.make_async_copy(x_ref, x_held, local_sem.at[1])
+    x_copy.start()
+
+    owner_hot = hot(iota((N_OWN, CLUSTERS), 0) == map_ref[...].reshape(1, CLUSTERS))
     earlier = hot(iota((CLUSTERS, CLUSTERS), 0) < iota((CLUSTERS, CLUSTERS), 1))
     before = dot(owner_hot, earlier)
     place = jnp.sum(owner_hot.astype(F32) * before, axis=0, keepdims=True)
     table = jnp.concatenate([owner_hot, jnp.broadcast_to(place, (16, CLUSTERS)).astype(BF16)], axis=0)
-    looked_up = dot(table, hot(iota((CLUSTERS, R_DEV), 0) == cid_ref[...]))
+    looked_up = dot(table, hot(iota((CLUSTERS, R_DEV), 0) == cid_ref[...].reshape(1, R_DEV)))
     row_hot, row_place = looked_up[:N_OWN], looked_up[N_OWN : N_OWN + 1]
     ahead = hot(iota((R_DEV, R_DEV), 0) < iota((R_DEV, R_DEV), 1))
     rank = jnp.sum(row_hot * dot(row_hot.astype(BF16), ahead), axis=0, keepdims=True)
     owner = jnp.sum(row_hot * iota((N_OWN, R_DEV), 0).astype(F32), axis=0, keepdims=True)
     rank = rank.astype(jnp.int32)
-    slot = owner.astype(jnp.int32) * CAP + rank
+    slot = step_to(me, owner.astype(jnp.int32)) * CAP + rank
     rank_hot = hot(iota((128, R_DEV), 0) == rank)
     rowhot_ref[...] = row_hot
     rank_ref[...] = rank_hot
     ids = dot_t((row_hot * (row_place + 1.0)).astype(BF16), rank_hot) - 1.0
-    for o in range(N_OWN):
-        ids_out[o] = jnp.broadcast_to(ids[o : o + 1], (8, 128))
-
-    x = x_ref[...]
+    ids_out[:, 0, :] = ids
+
+    x_copy.wait()
+    x = x_held[...]
     u = x * lax.rsqrt(jnp.sum(x * x, axis=1, keepdims=True) + 1e-06)
     high = u.astype(BF16)
     low = (u - high.astype(F32)).astype(BF16)
-    block = SLOTS // 4
-    for k in range(4):
+    block = SLOTS // PACKS
+
+    def pack(k):
         pick = hot(iota((block, R_DEV), 0) + k * block == slot)
         packed[pl.ds(k * block, block)] = dot(pick, high) + dot(pick, low)
 
+    pack(0)
+
+    @pl.when(home)
+    def _():
+        pl.semaphore_wait(barrier, MSGS - 1)
+
+    @pl.when(jnp.logical_not(home))
+    def _():
+        pl.semaphore_wait(barrier, N_OWN + 8)
+
     def at_slot(m):
         return pl.ds(pl.multiple_of(m * CAP, CAP), CAP)
 
     def send(i):
-        o = lax.rem(me + lax.rem(STEP * i, N_OWN), N_OWN)
+        o = partner(me, i)
         to = home_row(o)
         here = (o == me) & (to == grp)
         via, place = in_transit(me, grp, o)
@@ -132,24 +204,24 @@
         @pl.when(jnp.logical_not(here | via))
         def _():
             pltpu.make_async_remote_copy(
-                src_ref=packed.at[at_slot(o)], dst_ref=land.at[at_slot(m)], send_sem=send_sem.at[i],
+                src_ref=packed.at[at_slot(i)], dst_ref=land.at[at_slot(m)], send_sem=send_sem.at[i],
                 recv_sem=recv_sem.at[i // N_GRP], device_id=(to, o), device_id_type=MESH,
             ).start()
 
         @pl.when(via)
         def _():
             pltpu.make_async_remote_copy(
-                src_ref=packed.at[at_slot(o)], dst_ref=transit.at[at_slot(place)], send_sem=send_sem.at[i],
+                src_ref=packed.at[at_slot(i)], dst_ref=transit.at[at_slot(place)], send_sem=send_sem.at[i],
                 recv_sem=transit_sem.at[i], device_id=(grp, o), device_id_type=MESH,
             ).start()
 
         @pl.when(here)
         def _():
             pltpu.make_async_copy(ids_out.at[o], ids_in.at[m], local_sem.at[0]).start()
-            pltpu.make_async_copy(packed.at[at_slot(o)], land.at[at_slot(m)], send_sem.at[i]).start()
+            pltpu.make_async_copy(packed.at[at_slot(i)], land.at[at_slot(m)], send_sem.at[i]).start()
 
     def pass_on(i):
-        source = lax.rem(me + N_OWN - lax.rem(STEP * i, N_OWN), N_OWN)
+        source = partner(me, i, back=True)
         via, place = in_transit(source, grp, me)
 
         @pl.when(via)
@@ -164,28 +236,27 @@
     def sent(i):
         pltpu.make_async_copy(packed.at[at_slot(0)], packed.at[at_slot(0)], send_sem.at[i]).wait()
 
-    @pl.when(home)
-    def _():
-        lax.fori_loop(0, N_OWN, lambda i, _: (send(i), 0)[1], 0)
-
-    @pl.when(jnp.logical_not(home))
-    def _():
-        def step(i, _):
-            @pl.when((i >= WINDOW) & (i < N_OWN + WINDOW))
-            def _():
-                sent(i - WINDOW)
-
-            @pl.when(i < N_OWN)
-            def _():
-                send(i)
-
-            @pl.when((i >= LAG) & (i < N_OWN + LAG))
-            def _():
-                pass_on(i - LAG)
-
-            return 0
-
-        lax.fori_loop(0, N_OWN + max(WINDOW, LAG), step, 0)
+    def step(i, _):
+        @pl.when(jnp.logical_not(home) & (i >= WINDOW) & (i < N_OWN + WINDOW))
+        def _():
+            sent(i - WINDOW)
+
+        @pl.when(i < N_OWN)
+        def _():
+            send(i)
+
+        @pl.when((i >= LAG) & (i < N_OWN + LAG))
+        def _():
+            pass_on(i - LAG)
+
+        return 0
+
+    for k in range(PACKS):
+        if k:
+            pack(k)
+        group = N_OWN // PACKS
+        lax.fori_loop(k * group, (k + 1) * group, step, 0)
+    lax.fori_loop(N_OWN, N_OWN + max(WINDOW, LAG), step, 0)
 
     def wait(ref, count, sem):
         pltpu.make_async_copy(ref.at[pl.ds(0, count)], ref.at[pl.ds(0, count)], sem).wait()
@@ -208,7 +279,7 @@
             for t in range(CHUNK // 128):
                 lanes = pl.ds(right + t * 128, 128)
                 scaled = scores[:, t * 128 : (t + 1) * 128] * left_scale * scale_row[0:1, lanes]
-                weights = jnp.exp(scaled - SHARPNESS)
+                weights = jnp.exp(scaled)
                 same = left_ids == id_row[0:1, lanes]
                 weights = jnp.where(same, weights, 0.0)
                 total = total + weights
@@ -225,15 +296,15 @@
         row_acc[...] = jnp.zeros_like(row_acc)
         col_acc[...] = jnp.zeros_like(col_acc)
         wait(ids_out, 1, local_sem.at[0])
-        sent(0)
-
-        def chunk(a, _):
-            @pl.when(a == 0)
+        sent(SELF)
+
+        def prepare(a):
+            @pl.when(a == SELF // N_GRP)
             def _():
-                wait(ids_in, CHUNK_MSGS - 1, ids_recv_sem.at[0])
-                wait(land, CHUNK - CAP, recv_sem.at[0])
-
-            @pl.when(a > 0)
+                wait(ids_in, CHUNK_MSGS - 1, ids_recv_sem.at[SELF // N_GRP])
+                wait(land, CHUNK - CAP, recv_sem.at[SELF // N_GRP])
+
+            @pl.when(a != SELF // N_GRP)
             def _():
                 wait(ids_in, CHUNK_MSGS, ids_recv_sem.at[a])
                 wait(land, CHUNK, recv_sem.at[a])
@@ -261,13 +332,25 @@
             id_col[rows] = dot(picked, jnp.ones((128, 128), BF16))
             member = hot(iota((CL_OWN, CHUNK), 0).astype(F32) == row[0:1])
             sums[...] += dot(member, high) + dot(member, low)
+
+        def chunk(a, _):
+            prepare(a)
             lax.fori_loop(0, a, lambda b, _: (pair(a, b, False), 0)[1], 0)
             pair(a, a, True)
             return 0
 
-        lax.fori_loop(0, CHUNKS, chunk, 0)
-
-        def give_back(a, _):
+        last = CHUNKS - 1
+        lax.fori_loop(0, last, chunk, 0)
+        prepare(last)
+        total = sums[...]
+        cen_ref[...] = total * lax.rsqrt(jnp.mean(total * total, axis=1, keepdims=True) + 1e-06)
+        for k in range(1, N_GRP):
+            pltpu.make_async_remote_copy(
+                src_ref=cen_ref, dst_ref=cen_in, send_sem=cen_send_sem.at[k - 1], recv_sem=cen_recv_sem,
+                device_id=(lax.rem(grp + k, N_GRP), me), device_id_type=MESH,
+            ).start()
+
+        def give_back(a):
             rows = pl.ds(pl.multiple_of(a * CHUNK, CHUNK), CHUNK)
             part = row_acc[rows]
             high, middle, low = split3(part)
@@ -275,12 +358,11 @@
             mass = dot_t(ones, high) + (dot_t(ones, middle) + dot_t(ones, low))
             mass = mass[0:1] + jnp.sum(col_acc[:, rows], axis=0, keepdims=True)
             back = exact(dot_t, jnp.where(mine, mass, 0.0), spread)
-            for j in range(CHUNK_MSGS):
-                mass_out[a * CHUNK_MSGS + j] = jnp.broadcast_to(back[j : j + 1], (8, 128))
+            mass_out[pl.ds(a * CHUNK_MSGS, CHUNK_MSGS), 0, :] = back
             for j in range(CHUNK_MSGS):
                 i = a * (CHUNK_MSGS // N_GRP) + j // N_GRP
                 to_grp = j % N_GRP
-                to = lax.rem(me + N_OWN - lax.rem(STEP * i, N_OWN), N_OWN)
+                to = partner(me, i, back=True)
                 here = (to == me) & (grp == to_grp)
 
                 @pl.when(jnp.logical_not(here))
@@ -294,23 +376,21 @@
                 def _():
                     pltpu.make_async_copy(mass_out.at[a * CHUNK_MSGS + j], mass_in.at[me], local_sem.at[2]).start()
 
+        def finish(b, _):
+            pair(last, b, False)
+            give_back(b)
             return 0
 
-        lax.fori_loop(0, CHUNKS, give_back, 0)
-
-        total = sums[...]
-        cen_ref[...] = total * lax.rsqrt(jnp.mean(total * total, axis=1, keepdims=True) + 1e-06)
-        for k in range(1, N_GRP):
-            pltpu.make_async_remote_copy(
-                src_ref=cen_ref, dst_ref=cen_in, send_sem=cen_send_sem.at[k - 1], recv_sem=cen_recv_sem,
-                device_id=(lax.rem(grp + k, N_GRP), me), device_id_type=MESH,
-            ).start()
+        lax.fori_loop(0, last, finish, 0)
+        pair(last, last, True)
+        give_back(last)
+
         for k in range(1, N_GRP):
             pltpu.make_async_copy(cen_ref, cen_ref, cen_send_sem.at[k - 1]).wait()
         wait(mass_out, MSGS - 1, back_send_sem)
         wait(mass_out, 1, local_sem.at[2])
         wait(mass_in, N_OWN - 1, back_recv_sem)
-        lax.fori_loop(1, N_OWN, lambda i, _: (sent(i), 0)[1], 0)
+        lax.fori_loop(0, N_OWN - 1, lambda i, _: (sent(lax.rem(SELF + 1 + i, N_OWN)), 0)[1], 0)
         wait(ids_out, N_OWN - 1, ids_send_sem)
 
     @pl.when(jnp.logical_not(home))
@@ -327,9 +407,9 @@
 
     got = exact(dot, mass_in[:, 0, :], rank_ref[...])
     mass = jnp.sum(got * rowhot_ref[...], axis=0, keepdims=True)
-    score = jnp.broadcast_to(jnp.log(mass), (8, R_DEV))
-    target = hot(iota((R_DEV, R_DEV), 0) == order_ref[...])
-    dup_ref[...] = exact(dot_t, score, target)[0:1]
+    score = jnp.broadcast_to(jnp.log(mass) - SHARPNESS, (8, R_DEV))
+    target = hot(iota((R_DEV, R_DEV), 0) == order_ref[...].reshape(1, R_DEV))
+    dup_ref[...] = exact(dot_t, score, target)[0:1].reshape(R_DEV)
 
 
 def local(embeddings, cluster_ids, owner_map, source_order):
@@ -337,14 +417,14 @@
     dma = pltpu.SemaphoreType.DMA
     dup, centroids = pl.pallas_call(
         kernel,
-        out_shape=(jax.ShapeDtypeStruct((1, R_DEV), F32), jax.ShapeDtypeStruct((CL_OWN, D), F32)),
-        in_specs=[vmem] * 4,
+        out_shape=(jax.ShapeDtypeStruct((R_DEV,), F32), jax.ShapeDtypeStruct((CL_OWN, D), F32)),
+        in_specs=[pl.BlockSpec(memory_space=pl.ANY)] + [vmem] * 3,
         out_specs=(vmem, vmem),
         scratch_shapes=[
             pltpu.VMEM((SLOTS, D), F32),
-            pltpu.VMEM((N_OWN, 8, 128), F32),
+            pltpu.VMEM((N_OWN, 1, 128), F32),
             pltpu.VMEM((MSGS * CAP, D), F32),
-            pltpu.VMEM((MSGS, 8, 128), F32),
+            pltpu.VMEM((MSGS, 1, 128), F32),
             pltpu.VMEM((MSGS * CAP, D), BF16),
             pltpu.VMEM((MSGS * CAP, 128), F32),
             pltpu.VMEM((8, MSGS * CAP), F32),
@@ -355,21 +435,22 @@
             pltpu.VMEM((CL_OWN, D), F32),
             pltpu.VMEM((N_OWN, R_DEV), F32),
             pltpu.VMEM((128, R_DEV), BF16),
-            pltpu.VMEM((MSGS, 8, 128), F32),
-            pltpu.VMEM((N_OWN, 8, 128), F32),
+            pltpu.VMEM((MSGS, 1, 128), F32),
+            pltpu.VMEM((N_OWN, 1, 128), F32),
             pltpu.VMEM((CL_OWN, D), F32),
             pltpu.VMEM((16 * CAP, D), F32),
+            pltpu.VMEM((R_DEV, D), F32),
             dma((N_OWN,)), dma((N_OWN,)), dma, dma, dma((CHUNKS,)), dma((CHUNKS,)), dma((3,)), dma, dma, dma((3,)), dma,
         ],
-        compiler_params=pltpu.CompilerParams(has_side_effects=True, vmem_limit_bytes=60 << 20),
+        compiler_params=pltpu.CompilerParams(collective_id=0, has_side_effects=True, vmem_limit_bytes=60 << 20),
         name="owner_gather",
     )(
         embeddings,
-        cluster_ids.reshape(1, R_DEV),
-        owner_map.reshape(1, CLUSTERS),
-        source_order.reshape(1, R_DEV),
+        cluster_ids,
+        owner_map,
+        source_order,
     )
-    return dup.reshape(R_DEV), centroids
+    return dup, centroids
 
 
 def solution(mesh):

time: 153 us -> 141 us (0.922)
  Pallas kernels: 146 us -> 138 us
    pallas_call x1, Pallas kernels: 146 us -> 138 us  [local(): pl.pallas_call(kernel, out_shape=(jax.ShapeDtypeStruct((R_DEV,), F32), ja...]
    reshape x2 -> x0, local copies, waits for them, and re-layouts: 2.53 us -> none  [the longest x1 1.27 us: local(): cluster_ids.reshape(1, R_DEV)]
where the time goes in v3:
time: 141 us
  Pallas kernels  138 us (98%)
  local copies, waits for them, and re-layouts  2.69 us (2%)
    pallas_call x1, Pallas kernels, local(): pl.pallas_call(kernel, out_shape=(jax.ShapeDtypeStruct((R_DEV,), F32), ja...  138 us

profile of v3, /device:TPU:1, one launch (start us, length us, event | category | flops | bytes accessed | tf_op | source)
XLA Modules:
  0.0 141.0 jit_solution(2391176843393558948)
XLA Ops:
  0.6 137.6 %owner_gather.1 = (f32[768]{0:T(1024)}, f32[16,768]{1,0:T(8,128)}) custom-call(f32[768,768]{1,0:T(8,128)} %x_ref.1, s32[768]{0:T(1024)} %cid_ref.1, s32[512]{0:T(512)} %map_ref.1, s32[768]{0:T(1024)} %order_ref.1), custom_call_target="tpu_custom_call" | custom-call | tf_op jit(solution)/shard_map/owner_gather/pallas_call | solution.py:418
  138.3 1.3 copy.8
  139.5 1.4 %copy.9 = f32[16,768]{1,0:T(8,128)} copy(f32[16,768]{1,0:T(8,128)} %get-tuple-element.5) | data formatting | bytes 98304

commit v4 on v3

--- a/solution.py
+++ b/solution.py
@@ -24,10 +24,13 @@
 CHUNK = CHUNK_MSGS * CAP
 CHUNKS = MSGS // CHUNK_MSGS
 SHARPNESS = 6.0
+RELAYED = (4, 7)
 SELF = 31
-WINDOW = 8
+SELF_CHUNK = 6
+WINDOW = 12
 PACKS = 4
-LAG = 3
+PART = 256
+LAG = 5
 
 
 def hot(condition):
@@ -59,8 +62,9 @@
 
 
 def exact(product, a, b):
-    high, middle, low = split3(a)
-    return product(high, b) + (product(middle, b) + product(low, b))
+    rows = a.shape[0]
+    out = product(jnp.concatenate(split3(a), axis=0), b)
+    return out[:rows] + (out[rows : 2 * rows] + out[2 * rows :])
 
 
 def home_row(owner):
@@ -95,10 +99,33 @@
     return via, late * 8 + source // 8 * 2 + lax.rem(source, 2)
 
 
+def place_of(i, y_step):
+    group, a = i // 4, lax.rem(i, 4)
+    via = ((a == 0) & (lax.rem(y_step, 2) == 1)) | ((a == 1) & (y_step == 3)) | ((a == 2) & (y_step == 1))
+    early = jnp.where(
+        a == 0, y_step // 2, jnp.where(a == 1, 2 + y_step, jnp.where(a == 2, 5 + jnp.maximum(y_step - 1, 0), 8 + y_step))
+    )
+    n = jnp.where(via, 4 * group + jnp.where(a == 0, y_step // 2, a + 1), 12 * group + early)
+    k = n // CHUNK_MSGS
+    late = jnp.where(k == 0, RELAYED[0], RELAYED[1])
+    k = jnp.where(via, late, k + jnp.where(k >= RELAYED[0], 1, 0))
+    return k * CHUNK_MSGS + lax.rem(n, CHUNK_MSGS)
+
+
+def messages():
+    early, late = [], []
+    for i in range(N_OWN):
+        for y_step in range(N_GRP):
+            via = (i % 4, y_step) in ((0, 1), (0, 3), (1, 3), (2, 1))
+            (late if via else early).append((i, y_step))
+    first = RELAYED[0] * CHUNK_MSGS
+    return early[:first] + late[:CHUNK_MSGS] + early[first:] + late[CHUNK_MSGS:]
+
+
 def kernel(
     x_ref, cid_ref, map_ref, order_ref, dup_ref, cen_ref,
     packed, ids_out, land, ids_in, unit, row_acc, col_acc, id_col, id_row, scale_col, scale_row, sums, rowhot_ref, rank_ref,
-    mass_out, mass_in, cen_in, transit, x_held,
+    mass_out, mass_in, cen_in, transit, x_held, target_ref,
     send_sem, transit_sem, pass_sem, ids_send_sem, recv_sem, ids_recv_sem, local_sem, back_send_sem, back_recv_sem, cen_send_sem, cen_recv_sem,
 ):
     me, grp = lax.axis_index("own"), lax.axis_index("grp")
@@ -192,20 +219,21 @@
         to = home_row(o)
         here = (o == me) & (to == grp)
         via, place = in_transit(me, grp, o)
-        m = i * N_GRP + grp
+        m = place_of(i, lax.rem(to - grp + N_GRP, N_GRP))
+        part = m // CHUNK_MSGS
 
         @pl.when(jnp.logical_not(here))
         def _():
             pltpu.make_async_remote_copy(
                 src_ref=ids_out.at[o], dst_ref=ids_in.at[m], send_sem=ids_send_sem,
-                recv_sem=ids_recv_sem.at[i // N_GRP], device_id=(to, o), device_id_type=MESH,
+                recv_sem=ids_recv_sem.at[part], device_id=(to, o), device_id_type=MESH,
             ).start()
 
         @pl.when(jnp.logical_not(here | via))
         def _():
             pltpu.make_async_remote_copy(
                 src_ref=packed.at[at_slot(i)], dst_ref=land.at[at_slot(m)], send_sem=send_sem.at[i],
-                recv_sem=recv_sem.at[i // N_GRP], device_id=(to, o), device_id_type=MESH,
+                recv_sem=recv_sem.at[part], device_id=(to, o), device_id_type=MESH,
             ).start()
 
         @pl.when(via)
@@ -226,11 +254,12 @@
 
         @pl.when(via)
         def _():
+            m = place_of(i, lax.rem(home_row(me) - grp + N_GRP, N_GRP))
             here = transit.at[at_slot(place)]
             pltpu.make_async_copy(here, here, transit_sem.at[i]).wait()
             pltpu.make_async_remote_copy(
-                src_ref=here, dst_ref=land.at[at_slot(i * N_GRP + grp)], send_sem=pass_sem,
-                recv_sem=recv_sem.at[i // N_GRP], device_id=(home_row(me), me), device_id_type=MESH,
+                src_ref=here, dst_ref=land.at[at_slot(m)], send_sem=pass_sem,
+                recv_sem=recv_sem.at[m // CHUNK_MSGS], device_id=(home_row(me), me), device_id_type=MESH,
             ).start()
 
     def sent(i):
@@ -261,34 +290,39 @@
     def wait(ref, count, sem):
         pltpu.make_async_copy(ref.at[pl.ds(0, count)], ref.at[pl.ds(0, count)], sem).wait()
 
+    target_ref[...] = hot(iota((R_DEV, R_DEV), 0) == order_ref[...].reshape(1, R_DEV))
     cols = iota((128, CHUNK), 1)
     spread = hot(cols - CAP * by_48(cols) == iota((128, CHUNK), 0))
     mine = by_48(iota((CHUNK_MSGS, CHUNK), 1)) == iota((CHUNK_MSGS, CHUNK), 0)
 
-    def pair(a, b, diagonal):
+    def weigh(rows, right, width, only_rows):
+        scores = dot_t(unit[rows], unit[pl.ds(right, width)])
+        left_ids, left_scale, total = id_col[rows], scale_col[rows], row_acc[rows]
+        columns = []
+        for t in range(width // 128):
+            lanes = pl.ds(right + t * 128, 128)
+            weights = jnp.exp(scores[:, t * 128 : (t + 1) * 128] * left_scale * scale_row[0:1, lanes])
+            weights = jnp.where(left_ids == id_row[0:1, lanes], weights, 0.0)
+            total = total + weights
+            if t < only_rows:
+                columns.append(jnp.sum(weights.reshape(PART // 8, 8, 128), axis=0))
+        row_acc[rows] = total
+        return columns
+
+    def add_columns(right, columns):
+        for t, column in enumerate(columns):
+            col_acc[:, pl.ds(right + t * 128, 128)] += column
+
+    def pair(a, b):
         left = pl.multiple_of(a * CHUNK, CHUNK)
         right = pl.multiple_of(b * CHUNK, CHUNK)
-        part = 256
-        cols_sum = [jnp.zeros((8, 128), F32)] * (CHUNK // 128)
-        for r in range(CHUNK // part):
-            rows = pl.ds(left + r * part, part)
-            scores = dot_t(unit[rows], unit[pl.ds(right, CHUNK)])
-            left_ids = id_col[rows]
-            left_scale = scale_col[rows]
-            total = row_acc[rows]
-            for t in range(CHUNK // 128):
-                lanes = pl.ds(right + t * 128, 128)
-                scaled = scores[:, t * 128 : (t + 1) * 128] * left_scale * scale_row[0:1, lanes]
-                weights = jnp.exp(scaled)
-                same = left_ids == id_row[0:1, lanes]
-                weights = jnp.where(same, weights, 0.0)
-                total = total + weights
-                if not diagonal:
-                    cols_sum[t] = cols_sum[t] + jnp.sum(weights.reshape(part // 8, 8, 128), axis=0)
-            row_acc[rows] = total
-        if not diagonal:
-            for t in range(CHUNK // 128):
-                col_acc[:, pl.ds(right + t * 128, 128)] += cols_sum[t]
+        parts = [weigh(pl.ds(left + r * PART, PART), right, CHUNK, CHUNK // 128) for r in range(CHUNK // PART)]
+        add_columns(right, [sum(each) for each in zip(*parts)])
+
+    def inner(a):
+        left = pl.multiple_of(a * CHUNK, CHUNK)
+        for r in range(CHUNK // PART):
+            add_columns(left, weigh(pl.ds(left + r * PART, PART), left, (r + 1) * PART, r * PART // 128))
 
     @pl.when(home)
     def _():
@@ -299,12 +333,12 @@
         sent(SELF)
 
         def prepare(a):
-            @pl.when(a == SELF // N_GRP)
+            @pl.when(a == SELF_CHUNK)
             def _():
-                wait(ids_in, CHUNK_MSGS - 1, ids_recv_sem.at[SELF // N_GRP])
-                wait(land, CHUNK - CAP, recv_sem.at[SELF // N_GRP])
-
-            @pl.when(a != SELF // N_GRP)
+                wait(ids_in, CHUNK_MSGS - 1, ids_recv_sem.at[SELF_CHUNK])
+                wait(land, CHUNK - CAP, recv_sem.at[SELF_CHUNK])
+
+            @pl.when(a != SELF_CHUNK)
             def _():
                 wait(ids_in, CHUNK_MSGS, ids_recv_sem.at[a])
                 wait(land, CHUNK, recv_sem.at[a])
@@ -335,8 +369,8 @@
 
         def chunk(a, _):
             prepare(a)
-            lax.fori_loop(0, a, lambda b, _: (pair(a, b, False), 0)[1], 0)
-            pair(a, a, True)
+            lax.fori_loop(0, a, lambda b, _: (pair(a, b), 0)[1], 0)
+            inner(a)
             return 0
 
         last = CHUNKS - 1
@@ -350,8 +384,10 @@
                 device_id=(lax.rem(grp + k, N_GRP), me), device_id_type=MESH,
             ).start()
 
+        order = messages()
+
         def give_back(a):
-            rows = pl.ds(pl.multiple_of(a * CHUNK, CHUNK), CHUNK)
+            rows = pl.ds(a * CHUNK, CHUNK)
             part = row_acc[rows]
             high, middle, low = split3(part)
             ones = jnp.ones((8, 128), BF16)
@@ -360,30 +396,24 @@
             back = exact(dot_t, jnp.where(mine, mass, 0.0), spread)
             mass_out[pl.ds(a * CHUNK_MSGS, CHUNK_MSGS), 0, :] = back
             for j in range(CHUNK_MSGS):
-                i = a * (CHUNK_MSGS // N_GRP) + j // N_GRP
-                to_grp = j % N_GRP
+                i, y_step = order[a * CHUNK_MSGS + j]
+                to_grp = lax.rem(grp + N_GRP - y_step, N_GRP)
                 to = partner(me, i, back=True)
-                here = (to == me) & (grp == to_grp)
-
-                @pl.when(jnp.logical_not(here))
-                def _():
+                here = (i, y_step) == (SELF, 0)
+
+                block = mass_out.at[a * CHUNK_MSGS + j]
+                if here:
+                    pltpu.make_async_copy(block, mass_in.at[me], local_sem.at[2]).start()
+                else:
                     pltpu.make_async_remote_copy(
-                        src_ref=mass_out.at[a * CHUNK_MSGS + j], dst_ref=mass_in.at[me], send_sem=back_send_sem,
+                        src_ref=block, dst_ref=mass_in.at[me], send_sem=back_send_sem,
                         recv_sem=back_recv_sem, device_id=(to_grp, to), device_id_type=MESH,
                     ).start()
 
-                @pl.when(here)
-                def _():
-                    pltpu.make_async_copy(mass_out.at[a * CHUNK_MSGS + j], mass_in.at[me], local_sem.at[2]).start()
-
-        def finish(b, _):
-            pair(last, b, False)
-            give_back(b)
-            return 0
-
-        lax.fori_loop(0, last, finish, 0)
-        pair(last, last, True)
-        give_back(last)
+        lax.fori_loop(0, last, lambda b, _: (pair(last, b), 0)[1], 0)
+        inner(last)
+        for a in range(CHUNKS):
+            give_back(a)
 
         for k in range(1, N_GRP):
             pltpu.make_async_copy(cen_ref, cen_ref, cen_send_sem.at[k - 1]).wait()
@@ -407,9 +437,8 @@
 
     got = exact(dot, mass_in[:, 0, :], rank_ref[...])
     mass = jnp.sum(got * rowhot_ref[...], axis=0, keepdims=True)
-    score = jnp.broadcast_to(jnp.log(mass) - SHARPNESS, (8, R_DEV))
-    target = hot(iota((R_DEV, R_DEV), 0) == order_ref[...].reshape(1, R_DEV))
-    dup_ref[...] = exact(dot_t, score, target)[0:1].reshape(R_DEV)
+    score = jnp.broadcast_to(jnp.log(mass) - SHARPNESS, (16, R_DEV))
+    dup_ref[...] = exact(dot_t, score, target_ref[...])[0:1].reshape(R_DEV)
 
 
 def local(embeddings, cluster_ids, owner_map, source_order):
@@ -440,6 +469,7 @@
             pltpu.VMEM((CL_OWN, D), F32),
             pltpu.VMEM((16 * CAP, D), F32),
             pltpu.VMEM((R_DEV, D), F32),
+            pltpu.VMEM((R_DEV, R_DEV), BF16),
             dma((N_OWN,)), dma((N_OWN,)), dma, dma, dma((CHUNKS,)), dma((CHUNKS,)), dma((3,)), dma, dma, dma((3,)), dma,
         ],
         compiler_params=pltpu.CompilerParams(collective_id=0, has_side_effects=True, vmem_limit_bytes=60 << 20),

time: 141 us -> 138 us (0.979)
  Pallas kernels: 138 us -> 135 us
    pallas_call x1, Pallas kernels: 138 us -> 135 us  [local(): pl.pallas_call(kernel, out_shape=(jax.ShapeDtypeStruct((R_DEV,), F32), ja...]
where the time goes in v4:
time: 138 us
  Pallas kernels  135 us (98%)
  local copies, waits for them, and re-layouts  2.69 us (2%)
    pallas_call x1, Pallas kernels, local(): pl.pallas_call(kernel, out_shape=(jax.ShapeDtypeStruct((R_DEV,), F32), ja...  135 us

profile of v4, /device:TPU:1, one launch (start us, length us, event | category | flops | bytes accessed | tf_op | source)
XLA Modules:
  0.0 137.8 jit_solution(3755648737533402383)
XLA Ops:
  0.6 134.5 %owner_gather.1 = (f32[768]{0:T(1024)}, f32[16,768]{1,0:T(8,128)}) custom-call(f32[768,768]{1,0:T(8,128)} %x_ref.1, s32[768]{0:T(1024)} %cid_ref.1, s32[512]{0:T(512)} %map_ref.1, s32[768]{0:T(1024)} %order_ref.1), custom_call_target="tpu_custom_call" | custom-call | tf_op jit(solution)/shard_map/owner_gather/pallas_call | solution.py:447
  135.1 1.3 copy.8
  136.4 1.4 %copy.9 = f32[16,768]{1,0:T(8,128)} copy(f32[16,768]{1,0:T(8,128)} %get-tuple-element.5) | data formatting | bytes 98304

commit v5 on v4

--- a/solution.py
+++ b/solution.py
@@ -27,7 +27,7 @@
 RELAYED = (4, 7)
 SELF = 31
 SELF_CHUNK = 6
-WINDOW = 12
+WINDOW = 9
 PACKS = 4
 PART = 256
 LAG = 5

time: 138 us -> 136 us (0.986)
  Pallas kernels: 135 us -> 133 us
    pallas_call x1, Pallas kernels: 135 us -> 133 us  [local(): pl.pallas_call(kernel, out_shape=(jax.ShapeDtypeStruct((R_DEV,), F32), ja...]
where the time goes in v5:
time: 136 us
  Pallas kernels  133 us (98%)
  local copies, waits for them, and re-layouts  2.69 us (2%)
    pallas_call x1, Pallas kernels, local(): pl.pallas_call(kernel, out_shape=(jax.ShapeDtypeStruct((R_DEV,), F32), ja...  133 us

profile of v5, /device:TPU:1, one launch (start us, length us, event | category | flops | bytes accessed | tf_op | source)
XLA Modules:
  0.0 136.1 jit_solution(1122631232079048083)
XLA Ops:
  0.6 132.8 %owner_gather.1 = (f32[768]{0:T(1024)}, f32[16,768]{1,0:T(8,128)}) custom-call(f32[768,768]{1,0:T(8,128)} %x_ref.1, s32[768]{0:T(1024)} %cid_ref.1, s32[512]{0:T(512)} %map_ref.1, s32[768]{0:T(1024)} %order_ref.1), custom_call_target="tpu_custom_call" | custom-call | tf_op jit(solution)/shard_map/owner_gather/pallas_call | solution.py:447
  133.4 1.3 copy.8
  134.7 1.4 %copy.9 = f32[16,768]{1,0:T(8,128)} copy(f32[16,768]{1,0:T(8,128)} %get-tuple-element.5) | data formatting | bytes 98304

commit v6 on v5

--- a/solution.py
+++ b/solution.py
@@ -30,7 +30,7 @@
 WINDOW = 9
 PACKS = 4
 PART = 256
-LAG = 5
+LAG = 4
 
 
 def hot(condition):

time: 136 us -> 138 us (1.015)
  no operation moved by 1% of the time
where the time goes in v6:
time: 138 us; the launch traced here: 137 us
  Pallas kernels  134 us (97%)
  local copies, waits for them, and re-layouts  2.69 us (2%)
    pallas_call x1, Pallas kernels, local(): pl.pallas_call(kernel, out_shape=(jax.ShapeDtypeStruct((R_DEV,), F32), ja...  134 us

profile of v6, /device:TPU:1, one launch (start us, length us, event | category | flops | bytes accessed | tf_op | source)
XLA Modules:
  0.0 137.4 jit_solution(646497630215699591)
XLA Ops:
  0.6 134.1 %owner_gather.1 = (f32[768]{0:T(1024)}, f32[16,768]{1,0:T(8,128)}) custom-call(f32[768,768]{1,0:T(8,128)} %x_ref.1, s32[768]{0:T(1024)} %cid_ref.1, s32[512]{0:T(512)} %map_ref.1, s32[768]{0:T(1024)} %order_ref.1), custom_call_target="tpu_custom_call" | custom-call | tf_op jit(solution)/shard_map/owner_gather/pallas_call | solution.py:447
  134.7 1.3 copy.8
  136.0 1.4 %copy.9 = f32[16,768]{1,0:T(8,128)} copy(f32[16,768]{1,0:T(8,128)} %get-tuple-element.5) | data formatting | bytes 98304
